TPU v7x, 256 devices: a whole 4x4x8 slice. The times are simulated.
256 devices in a mesh: slab: 8 (over y, core), trace: 32 (over x, z).
Axes of the slice: x: 4, y: 4, z: 8, core: 2. Of those that a mesh axis runs over, the one named last changes fastest.
Arguments:
- near_tiles: float32 [8, 2, 2, 768, 24576], P('slab', None, None, None, 'trace'), may hold values from -0.078125 to 0.078125
- near_side: int32 [8, 32], P('slab', 'trace'), may hold values from -1 to 1, as said below
- skeleton: int32 [8, 32, 64], P('slab', 'trace'), may hold values from 0 to 767, as said below
- far_coupling: float32 [8, 2, 2048, 2048], P('slab', None, 'trace'), may hold values from -0.0625 to 0.0625
- far_basis: float32 [8, 2, 64, 24576], P('slab', None, None, 'trace'), may hold values from -0.5 to 0.5
- sources: float32 [8, 2, 1, 16, 24576], P('slab', None, None, None, 'trace'), may hold values from -200 to 200
Outputs:
- traces: float32 [8, 2, 1, 16, 24576], P('slab', None, None, None, 'trace')
Inputs may be any that keep to these rules, and one draw needn't show every extreme that they name: `near_side`: each entry is -1 or 1, so that the second near tile lies in a block next to the row's own block; it is 1 for the first block and -1 for the last. `skeleton`: the 64 positions of one block are distinct.
All inputs are finite; a program needn't handle non-finite values.
Results may differ from a plain program's by a relative error of at most 0.0001.
Values sent between devices are 32-bit elements; how exact they have to be, the bound alone decides.
A program may use at most 128 MiB of HBM per device.

v0:
```python
import jax
import jax.numpy as jnp
from jax import lax
from jax.sharding import PartitionSpec as P

exact_mode = lax.Precision.HIGHEST
small_eps = 1e-06


def extended(block, sides, width):
    for axis, dim in sides:
        count = lax.axis_size(axis)
        forward = [(i, i + 1) for i in range(count - 1)]
        backward = [(target, source) for source, target in forward]
        low = lax.ppermute(
            lax.slice_in_dim(block, block.shape[dim] - width, None, axis=dim), axis, forward
        )
        high = lax.ppermute(lax.slice_in_dim(block, 0, width, axis=dim), axis, backward)
        block = jnp.concatenate([low, block, high], axis=dim)
    return block


def from_behind(x, axis, by):
    size = lax.axis_size(axis)
    pairs = [(i, i + by) for i in range(size) if 0 <= i + by < size]
    return lax.ppermute(x, axis, pairs)


def real_block(part_re, part_im):
    upper = jnp.concatenate([part_re, part_im], axis=1)
    lower = jnp.concatenate([-part_im, part_re], axis=1)
    return jnp.concatenate([upper, lower], axis=0)


def build_mats(tile_set, coupling, basis):
    near_mat = jnp.concatenate(
        [real_block(tile_set[0, 0], tile_set[0, 1]), real_block(tile_set[1, 0], tile_set[1, 1])],
        axis=0,
    )
    coef_mat = real_block(coupling[0].T, coupling[1].T)
    basis_mat = real_block(basis[0], basis[1])
    return (near_mat, coef_mat, basis_mat)


def apply_operator(trace_in, mats, offset, skel_index):
    near_mat, coef_mat, basis_mat = mats
    width = trace_in.shape[2]
    padded = extended(trace_in, (("trace", 2),), width)
    beside_in = lax.dynamic_slice_in_dim(padded, (1 + offset) * width, width, axis=2)
    stacked_in = jnp.concatenate([trace_in[0], trace_in[1], beside_in[0], beside_in[1]], axis=1)
    near_out = jnp.dot(stacked_in, near_mat, precision=exact_mode)
    picked = jnp.take(trace_in, skel_index, axis=2)
    gathered = lax.all_gather(picked, "trace", axis=2, tiled=True)
    rank_count = picked.shape[2]
    block_here = lax.axis_index("trace")
    owner_ids = jnp.arange(gathered.shape[2], dtype=jnp.int32) // rank_count
    keep_mask = ((owner_ids != block_here) & (owner_ids != block_here + offset)).astype(jnp.float32)
    masked = gathered * keep_mask
    coef_out = jnp.dot(
        jnp.concatenate([masked[0], masked[1]], axis=1), coef_mat, precision=exact_mode
    )
    far_out = jnp.dot(coef_out, basis_mat, precision=exact_mode)
    total = near_out + far_out
    return jnp.stack([total[:, :width], total[:, width:]])


def on_device(near_tiles, near_side, skeleton, far_coupling, far_basis, sources):
    mats = build_mats(near_tiles[0], far_coupling[0], far_basis[0])
    offset = near_side[0, 0]
    skel_index = skeleton[0, 0]
    local_src = sources[0]
    batches = local_src.shape[1]
    shots = local_src.shape[2]
    width = local_src.shape[3]
    slab_count = lax.axis_size("slab")
    all_src = local_src.reshape(2, batches * shots, width)
    trace_in = jnp.zeros_like(all_src)
    updated = all_src
    for step_idx in range(slab_count):
        updated = apply_operator(trace_in, mats, offset, skel_index) + all_src
        if step_idx + 1 < slab_count:
            trace_in = from_behind(updated, "slab", 1)
    finished = updated.reshape(2, batches, shots, width)
    partial_sum = jnp.sum(finished * finished, axis=(0, 3))
    total_sum = lax.psum(partial_sum, "trace")
    mean_square = total_sum / (2 * width * lax.axis_size("trace"))
    normed = finished / jnp.sqrt(mean_square + small_eps)[None, :, :, None]
    return normed[None]


def solution(mesh):
    placed = (
        P("slab", None, None, None, "trace"),
        P("slab", "trace"),
        P("slab", "trace", None),
        P("slab", None, "trace", None),
        P("slab", None, None, "trace"),
        P("slab", None, None, None, "trace"),
    )
    return jax.shard_map(
        on_device,
        mesh=mesh,
        in_specs=placed,
        out_specs=P("slab", None, None, None, "trace"),
        check_vma=False,
    )
```

profile of v0, /device:TPU:24, one launch (start us, length us, event | category | flops | bytes accessed | tf_op | source)
XLA Modules:
  0.0 850.5 jit_solution(1548529187683753555)
XLA Ops:
  0.0 4.6 collective-permute-start
  11.9 7.3 slice_bitcast_fusion.2
  22.7 59.9 %all_gather.24 = f32[2,16,2048]{1,0,2:T(2,128)} all-gather(f32[2,16,64]{1,0,2:T(2,128)S(1)} %select_bitcast_fusion.7), channel_id=1, replica_groups=mesh['slab'=8,'trace'=32] {'trace'}, dimensions={2}, use_global_device_ids=true | all-gather | bytes 270336 | tf_op jit(solution)/shard_map/all_gather | solution.py:53
  83.2 6.8 broadcast_multiply_fusion.7
  99.2 15.9 %maximum_maximum_fusion = f32[3072,1536]{1,0:T(8,128)} fusion(f32[768,768]{1,0:T(8,128)} %get-tuple-element.8, f32[768,768]{1,0:T(8,128)} %get-tuple-element.11, f32[768,768]{1,0:T(8,128)S(1)} %copy-done, f32[768,768]{1,0:T(8,128)} %get-tuple-element.9, f32[768,768]{1,0:T(8,128)} %get-tuple-element.10, f32[768,768]{1,0:T(8,128)S(1)} %get-tuple-element.6), kind=kLoop, calls=%fused_computation.8 | loop fusion | flops 33030144 | bytes 33030144 | tf_op jit(solution)/shard_map/concatenate | solution.py:36
  116.6 12.1 %convolution_add_fusion.7 = f32[16,1536]{1,0:T(8,128)S(1)} fusion(f32[16,1536]{1,0:T(8,128)S(1)} %fusion.139, f32[3072,1536]{1,0:T(8,128)} %maximum_maximum_fusion, f32[16,768]{1,0:T(8,128)S(1)} %get-tuple-element.79, f32[16,768]{1,0:T(8,128)S(1)} %get-tuple-element.78, f32[3072]{0:T(1024)S(1)} %pad.99.clone), kind=kOutput, calls=%fused_computation.20 | convolution fusion | flops 906092544 | bytes 19181568 | tf_op jit(solution)/shard_map/dot_general | solution.py:51
  135.9 51.0 %all_gather.25 = f32[2,16,2048]{1,0,2:T(2,128)S(1)} all-gather(f32[2,16,64]{1,0,2:T(2,128)S(1)} %select_bitcast_fusion.6), channel_id=1, replica_groups=mesh['slab'=8,'trace'=32] {'trace'}, dimensions={2}, use_global_device_ids=true | all-gather | bytes 270336 | tf_op jit(solution)/shard_map/all_gather | solution.py:53
  186.8 5.8 broadcast_multiply_fusion.6
  202.9 4.3 collective-permute-done.4
  207.3 12.1 %convolution_add_fusion.6 = f32[16,1536]{1,0:T(8,128)S(1)} fusion(f32[16,1536]{1,0:T(8,128)S(1)} %fusion.138, f32[3072,1536]{1,0:T(8,128)} %maximum_maximum_fusion, f32[16,768]{1,0:T(8,128)S(1)} %get-tuple-element.75, f32[16,768]{1,0:T(8,128)S(1)} %get-tuple-element.74, f32[16,768]{1,0:T(8,128)S(1)} %get-tuple-element.73, f32[16,768]{1,0:T(8,128)S(1)} %get-tuple-element.72), kind=kOutput, calls=%fused_computation.19 | convolution fusion | flops 906141696 | bytes 19267584 | tf_op jit(solution)/shard_map/dot_general | solution.py:51
  226.6 52.9 %all_gather.26 = f32[2,16,2048]{1,0,2:T(2,128)S(1)} all-gather(f32[2,16,64]{1,0,2:T(2,128)S(1)} %select_bitcast_fusion.5), channel_id=1, replica_groups=mesh['slab'=8,'trace'=32] {'trace'}, dimensions={2}, use_global_device_ids=true | all-gather | bytes 270336 | tf_op jit(solution)/shard_map/all_gather | solution.py:53
  279.4 5.8 broadcast_multiply_fusion.5
  295.2 4.3 collective-permute-done.7
  299.6 12.1 %convolution_add_fusion.5 = f32[16,1536]{1,0:T(8,128)S(1)} fusion(f32[16,1536]{1,0:T(8,128)S(1)} %fusion.137, f32[3072,1536]{1,0:T(8,128)} %maximum_maximum_fusion, f32[16,768]{1,0:T(8,128)S(1)} %get-tuple-element.69, f32[16,768]{1,0:T(8,128)S(1)} %get-tuple-element.68, f32[16,768]{1,0:T(8,128)S(1)} %get-tuple-element.67, f32[16,768]{1,0:T(8,128)S(1)} %get-tuple-element.66), kind=kOutput, calls=%fused_computation.18 | convolution fusion | flops 906141696 | bytes 19267584 | tf_op jit(solution)/shard_map/dot_general | solution.py:51
  318.9 54.6 %all_gather.27 = f32[2,16,2048]{1,0,2:T(2,128)S(1)} all-gather(f32[2,16,64]{1,0,2:T(2,128)S(1)} %select_bitcast_fusion.4), channel_id=1, replica_groups=mesh['slab'=8,'trace'=32] {'trace'}, dimensions={2}, use_global_device_ids=true | all-gather | bytes 270336 | tf_op jit(solution)/shard_map/all_gather | solution.py:53
  373.5 5.8 broadcast_multiply_fusion.4
  385.8 4.6 collective-permute-start.9
  392.6 12.1 %convolution_add_fusion.4 = f32[16,1536]{1,0:T(8,128)S(1)} fusion(f32[16,1536]{1,0:T(8,128)S(1)} %fusion.136, f32[3072,1536]{1,0:T(8,128)} %maximum_maximum_fusion, f32[16,768]{1,0:T(8,128)S(1)} %get-tuple-element.63, f32[16,768]{1,0:T(8,128)S(1)} %get-tuple-element.62, f32[16,768]{1,0:T(8,128)S(1)} %get-tuple-element.61, f32[16,768]{1,0:T(8,128)S(1)} %get-tuple-element.60), kind=kOutput, calls=%fused_computation.17 | convolution fusion | flops 906141696 | bytes 19267584 | tf_op jit(solution)/shard_map/dot_general | solution.py:51
  411.9 54.4 %all_gather.28 = f32[2,16,2048]{1,0,2:T(2,128)S(1)} all-gather(f32[2,16,64]{1,0,2:T(2,128)S(1)} %select_bitcast_fusion.3), channel_id=1, replica_groups=mesh['slab'=8,'trace'=32] {'trace'}, dimensions={2}, use_global_device_ids=true | all-gather | bytes 270336 | tf_op jit(solution)/shard_map/all_gather | solution.py:53
  466.3 5.8 broadcast_multiply_fusion.3
  485.8 12.1 %convolution_add_fusion.3 = f32[16,1536]{1,0:T(8,128)S(1)} fusion(f32[16,1536]{1,0:T(8,128)S(1)} %fusion.135, f32[3072,1536]{1,0:T(8,128)} %maximum_maximum_fusion, f32[16,768]{1,0:T(8,128)S(1)} %get-tuple-element.57, f32[16,768]{1,0:T(8,128)S(1)} %get-tuple-element.56, f32[16,768]{1,0:T(8,128)S(1)} %get-tuple-element.55, f32[16,768]{1,0:T(8,128)S(1)} %get-tuple-element.54), kind=kOutput, calls=%fused_computation.16 | convolution fusion | flops 906141696 | bytes 19267584 | tf_op jit(solution)/shard_map/dot_general | solution.py:51
  505.1 54.1 %all_gather.29 = f32[2,16,2048]{1,0,2:T(2,128)S(1)} all-gather(f32[2,16,64]{1,0,2:T(2,128)S(1)} %select_bitcast_fusion.2), channel_id=1, replica_groups=mesh['slab'=8,'trace'=32] {'trace'}, dimensions={2}, use_global_device_ids=true | all-gather | bytes 270336 | tf_op jit(solution)/shard_map/all_gather | solution.py:53
  559.2 5.8 broadcast_multiply_fusion.2
  578.3 12.1 %convolution_add_fusion.2 = f32[16,1536]{1,0:T(8,128)S(1)} fusion(f32[16,1536]{1,0:T(8,128)S(1)} %fusion.134, f32[3072,1536]{1,0:T(8,128)} %maximum_maximum_fusion, f32[16,768]{1,0:T(8,128)S(1)} %get-tuple-element.51, f32[16,768]{1,0:T(8,128)S(1)} %get-tuple-element.50, f32[16,768]{1,0:T(8,128)S(1)} %get-tuple-element.49, f32[16,768]{1,0:T(8,128)S(1)} %get-tuple-element.48), kind=kOutput, calls=%fused_computation.15 | convolution fusion | flops 906141696 | bytes 19267584 | tf_op jit(solution)/shard_map/dot_general | solution.py:51
  597.6 54.8 %all_gather.30 = f32[2,16,2048]{1,0,2:T(2,128)S(1)} all-gather(f32[2,16,64]{1,0,2:T(2,128)S(1)} %select_bitcast_fusion.1), channel_id=1, replica_groups=mesh['slab'=8,'trace'=32] {'trace'}, dimensions={2}, use_global_device_ids=true | all-gather | bytes 270336 | tf_op jit(solution)/shard_map/all_gather | solution.py:53
  652.4 5.8 broadcast_multiply_fusion.1
  667.3 4.3 collective-permute-done.19
  671.7 12.1 %convolution_add_fusion.1 = f32[16,1536]{1,0:T(8,128)S(1)} fusion(f32[16,1536]{1,0:T(8,128)S(1)} %fusion.133, f32[3072,1536]{1,0:T(8,128)} %maximum_maximum_fusion, f32[16,768]{1,0:T(8,128)S(1)} %get-tuple-element.45, f32[16,768]{1,0:T(8,128)S(1)} %get-tuple-element.44, f32[16,768]{1,0:T(8,128)S(1)} %get-tuple-element.43, f32[16,768]{1,0:T(8,128)S(1)} %get-tuple-element.42), kind=kOutput, calls=%fused_computation.14 | convolution fusion | flops 906141696 | bytes 19267584 | tf_op jit(solution)/shard_map/dot_general | solution.py:51
  691.0 54.7 %all_gather.31 = f32[2,16,2048]{1,0,2:T(2,128)S(1)} all-gather(f32[2,16,64]{1,0,2:T(2,128)S(1)} %select_bitcast_fusion), channel_id=1, replica_groups=mesh['slab'=8,'trace'=32] {'trace'}, dimensions={2}, use_global_device_ids=true | all-gather | bytes 270336 | tf_op jit(solution)/shard_map/all_gather | solution.py:53
  745.7 5.8 broadcast_multiply_fusion
  764.6 12.1 %convolution_add_fusion = f32[16,1536]{1,0:T(8,128)S(1)} fusion(f32[16,1536]{1,0:T(8,128)S(1)} %fusion.132, f32[3072,1536]{1,0:T(8,128)} %maximum_maximum_fusion, f32[16,768]{1,0:T(8,128)S(1)} %get-tuple-element.39, f32[16,768]{1,0:T(8,128)S(1)} %get-tuple-element.38, f32[16,768]{1,0:T(8,128)S(1)} %get-tuple-element.37, f32[16,768]{1,0:T(8,128)S(1)} %get-tuple-element.36), kind=kOutput, calls=%fused_computation.13 | convolution fusion | flops 906141696 | bytes 19267584 | tf_op jit(solution)/shard_map/dot_general | solution.py:51
  776.8 72.5 %psum.7 = f32[1,16]{1,0:T(1,128)S(1)} all-reduce(f32[1,16]{1,0:T(1,128)S(1)} %bitcast.213), channel_id=1, replica_groups=mesh['slab'=8,'trace'=32] {'trace'}, use_global_device_ids=true, to_apply=%region_1.3 | all-reduce | flops 16 | bytes 128 | tf_op jit(solution)/shard_map/psum | solution.py:85
  (225 shorter events, 150.7 us)
Async XLA Ops:
  0.0 9.6 %copy-start.2 = (f32[1,2,64,2048]{3,2,1,0:T(8,128)S(1)}, f32[1,2,64,2048]{3,2,1,0:T(8,128)}, u32[]{:S(2)}) copy-start(f32[1,2,64,2048]{3,2,1,0:T(8,128)} %param.11) | copy-start | bytes 3145732
  0.0 10.4 %copy-start.3 = (f32[1,2,64,768]{3,2,1,0:T(8,128)S(1)}, f32[1,2,64,768]{3,2,1,0:T(8,128)}, u32[]{:S(2)}) copy-start(f32[1,2,64,768]{3,2,1,0:T(8,128)} %param.12) | copy-start | bytes 1179652
  0.0 115.6 %collective-permute-start = (f32[2,16,768]{2,1,0:T(8,128)S(1)}, f32[2,16,768]{2,1,0:T(8,128)}, u32[]{:S(2)}, u32[]{:S(2)}) collective-permute-start(f32[2,16,768]{2,1,0:T(8,128)S(1)} %broadcast_in_dim.11), channel_id=1, source_target_pairs={{0,1},{1,2},{2,3},{3,4},{4,5},{5,6},{6,7},{7,8},{8,9},{9,10},{10,1... | collective-permute-start | bytes 294920 | tf_op jit(solution)/shard_map/ppermute | solution.py:15
  4.6 111.0 %collective-permute-start.1 = (f32[2,16,768]{2,1,0:T(8,128)S(1)}, f32[2,16,768]{2,1,0:T(8,128)}, u32[]{:S(2)}, u32[]{:S(2)}) collective-permute-start(f32[2,16,768]{2,1,0:T(8,128)S(1)} %broadcast_in_dim.11), channel_id=1, source_target_pairs={{1,0},{2,1},{3,2},{4,3},{5,4},{6,5},{7,6},{8,7},{9,8},{10,9},{11,1... | collective-permute-start | bytes 294920 | tf_op jit(solution)/shard_map/ppermute | solution.py:18
  99.2 15.9 %copy-start.6 = (f32[64,768]{1,0:T(8,128)S(1)}, f32[64,768]{1,0:T(8,128)}, u32[]{:S(2)}) copy-start(f32[64,768]{1,0:T(8,128)} %fusion.128) | copy-start | bytes 589828
  99.2 15.9 %copy-start.14 = (f32[64,768]{1,0:T(8,128)S(1)}, f32[64,768]{1,0:T(8,128)}, u32[]{:S(2)}) copy-start(f32[64,768]{1,0:T(8,128)} %get-tuple-element.30) | copy-start | bytes 589828
  99.2 15.9 %copy-start.22 = (f32[64,768]{1,0:T(8,128)S(1)}, f32[64,768]{1,0:T(8,128)}, u32[]{:S(2)}) copy-start(f32[64,768]{1,0:T(8,128)} %get-tuple-element.31) | copy-start | bytes 589828
  116.5 12.1 %copy-start.1 = (f32[1,2,1,16,768]{4,3,2,1,0:T(8,128)S(1)}, f32[1,2,1,16,768]{4,3,2,1,0:T(8,128)}, u32[]{:S(2)}) copy-start(f32[1,2,1,16,768]{4,3,2,1,0:T(8,128)} %param.13) | copy-start | bytes 294916
  128.7 5.9 collective-permute-start.2
  198.5 4.4 collective-permute-start.3
  200.7 6.5 collective-permute-start.4
  219.4 5.9 collective-permute-start.5
  290.5 4.7 collective-permute-start.6
  293.0 6.5 collective-permute-start.7
  311.7 5.9 collective-permute-start.8
  381.5 8.9 %copy-start.9 = (f32[64,768]{1,0:T(8,128)S(1)}, f32[64,768]{1,0:T(8,128)}, u32[]{:S(2)}) copy-start(f32[64,768]{1,0:T(8,128)} %fusion.128) | copy-start | bytes 589828
  381.5 8.9 %copy-start.17 = (f32[64,768]{1,0:T(8,128)S(1)}, f32[64,768]{1,0:T(8,128)}, u32[]{:S(2)}) copy-start(f32[64,768]{1,0:T(8,128)} %get-tuple-element.30) | copy-start | bytes 589828
  381.5 8.9 %copy-start.25 = (f32[64,768]{1,0:T(8,128)S(1)}, f32[64,768]{1,0:T(8,128)}, u32[]{:S(2)}) copy-start(f32[64,768]{1,0:T(8,128)} %get-tuple-element.31) | copy-start | bytes 589828
  384.5 6.5 collective-permute-start.10
  385.8 6.8 collective-permute-start.9
  404.7 5.9 collective-permute-start.11
  477.3 4.1 collective-permute-start.12
  479.2 6.5 collective-permute-start.13
  497.9 5.9 collective-permute-start.14
  570.2 3.7 collective-permute-start.15
  571.7 6.5 collective-permute-start.16
  590.4 5.9 collective-permute-start.17
  663.4 3.9 collective-permute-start.18
  665.2 6.5 collective-permute-start.19
  683.8 5.9 collective-permute-start.20
  756.7 3.5 collective-permute-start.21
  758.0 6.5 collective-permute-start.22
  (24 other events, 139.9 us)
where the time goes:
time: 860 us; the launch traced here: 851 us
  blocking collectives  509 us (59%)
  matrix products  125 us (15%)
  other arithmetic  71.5 us (8%)
  waiting for transfers between devices  58 us (7%)
  starting transfers between devices  44.1 us (5%)
  local copies, waits for them, and re-layouts  41.3 us (5%)
    all_gather x8, blocking collectives, apply_operator(): gathered = lax.all_gather(picked, 'trace', axis=2, tiled=True)  436 us
    dot_general x8, matrix products, apply_operator(): near_out = jnp.dot(stacked_in, near_mat, precision=exact_mode)  96.5 us
    psum x1, blocking collectives, on_device(): total_sum = lax.psum(partial_sum, 'trace')  72.5 us
    mul x8, other arithmetic, apply_operator(): masked = gathered * keep_mask  47.1 us
    ppermute x7, waiting for transfers between devices, from_behind(): return lax.ppermute(x, axis, pairs)  28.1 us
    ppermute x8, waiting for transfers between devices, extended(): lax.ppermute(lax.slice_in_dim(block, 0, width, axis=dim), axis, backward)  26.1 us
    dot_general x8, matrix products, apply_operator(): jnp.dot(jnp.concatenate([masked[0], masked[1]], axis=1), coef_mat, precis...  24.4 us
    ppermute x8, starting transfers between devices, extended(): lax.ppermute(lax.slice_in_dim(block, block.shape[dim] - width, None, axis...  20.3 us
  transfers between devices with their start and end apart: 23, of which 21 were waited for; matrix products, arithmetic and copies ran while one was open for 6% of the time, Pallas kernels for 0%

commit v1 on v0

v1 whole, which is shorter than its diff:
```python
import functools

import jax
import jax.numpy as jnp
from jax import lax
from jax.experimental import pallas as pl
from jax.experimental.pallas import tpu as pltpu
from jax.sharding import PartitionSpec as P

MESH = pl.DeviceIdType.MESH
F32 = jnp.float32
BF16 = jnp.bfloat16
small_eps = 1e-06


def halves(x):
    hi = x.astype(BF16)
    lo = (x - hi.astype(F32)).astype(BF16)
    return hi, lo


def thirds(x):
    hi = x.astype(BF16)
    rest = x - hi.astype(F32)
    mid = rest.astype(BF16)
    lo = (rest - mid.astype(F32)).astype(BF16)
    return hi, mid, lo


def mm(a, b):
    return jnp.dot(a, b, preferred_element_type=F32)


def outward(k, n):
    return (n // 2 + ((k + 1) // 2) * (1 - 2 * (k % 2))) % n


def kernel(
    sizes,
    near_hbm,
    side_ref,
    skel_ref,
    coup_hbm,
    basis_hbm,
    src_hbm,
    out_ref,
    near_f,
    near_hi,
    near_lo,
    coup_f,
    basis_f,
    basis_w,
    src_v,
    skel_out,
    skel_next,
    pick_w,
    wp,
    wc,
    u_in,
    u_out,
    p_in,
    p_out,
    e_in,
    e_out,
    w_sem,
    skel_sem,
    u_send,
    u_recv,
    p_send,
    p_recv,
    e_send,
    e_recv,
):
    ns, nt, nx, nz = sizes
    tile = src_v.shape[2]
    rows = src_v.shape[1]
    rank = skel_ref.shape[1]
    slab = lax.axis_index("slab")
    me = lax.axis_index("trace")
    my_x, my_z = me // nz, me % nz
    has_next = slab < ns - 1
    has_prev = slab > 0
    lane = lax.broadcasted_iota(jnp.int32, (rank, 2 * rank), 1)
    first = lane < rank

    loads = [
        pltpu.make_async_copy(src_hbm, src_v, w_sem.at[0]),
        pltpu.make_async_copy(basis_hbm, basis_f, w_sem.at[1]),
        pltpu.make_async_copy(coup_hbm, coup_f, w_sem.at[2]),
    ]
    for slot in range(2):
        for part in range(2):
            loads.append(
                pltpu.make_async_copy(
                    near_hbm.at[slot, part], near_f.at[slot, part], w_sem.at[3 + 2 * slot + part]
                )
            )
    for load in loads:
        load.start()

    barrier = pltpu.get_barrier_semaphore()

    def greet(s, t):
        pl.semaphore_signal(barrier, inc=1, device_id=(s, t), device_id_type=MESH)

    @pl.when(has_next)
    def _():
        greet(slab + 1, me)

    @pl.when(has_prev)
    def _():
        @pl.loop(0, nt)
        def _(k):
            greet(slab - 1, (me + nt // 2 + k) % nt)

    @pl.loop(1, nt)
    def _(k):
        greet(slab, (me + k) % nt)

    twin = jnp.concatenate([skel_ref[...], skel_ref[...]], axis=1)
    skel_out[...] = jnp.broadcast_to(twin, skel_out.shape)

    pl.semaphore_wait(
        barrier, nt - 1 + nt * has_next.astype(jnp.int32) + has_prev.astype(jnp.int32)
    )

    skel_copy = pltpu.make_async_remote_copy(
        src_ref=skel_out,
        dst_ref=skel_next,
        send_sem=skel_sem.at[0],
        recv_sem=skel_sem.at[1],
        device_id=(slab - 1, me),
        device_id_type=MESH,
    )

    @pl.when(has_prev)
    def _():
        skel_copy.start()

    def send_u():
        for i, shift in enumerate((0, 1, nt - 1)):
            pltpu.make_async_remote_copy(
                src_ref=u_out,
                dst_ref=u_in.at[i],
                send_sem=u_send.at[i],
                recv_sem=u_recv.at[i],
                device_id=(slab + 1, (me + shift) % nt),
                device_id_type=MESH,
            ).start()

    def send_p():
        @pl.loop(0, nt)
        def _(k):
            dz, dx = outward(k // nx, nz), outward(k % nx, nx)
            to = ((my_x + dx) % nx) * nz + (my_z + dz) % nz
            pltpu.make_async_remote_copy(
                src_ref=p_out,
                dst_ref=p_in.at[dz, my_x],
                send_sem=p_send,
                recv_sem=p_recv.at[dz],
                device_id=(slab + 1, to),
                device_id_type=MESH,
            ).start()

    def pick(x):
        parts = mm(jnp.concatenate(thirds(x), axis=0), pick_w[...])
        n = 2 * rows
        got = parts[:n] + parts[n : 2 * n] + parts[2 * n :]
        return jnp.where(first[:rows], got[:rows], got[rows:])

    @pl.when(has_next)
    def _():
        skel_copy.wait_recv()
        place = lax.broadcasted_iota(jnp.int32, (tile, 2 * rank), 0)
        pick_w[...] = (place == skel_next[:1, :]).astype(BF16)

    @pl.when(jnp.logical_not(has_next))
    def _():
        pick_w[...] = jnp.zeros_like(pick_w)

    loads[0].wait()

    @pl.when(slab == 0)
    def _():
        u_out[...] = src_v[...]
        p_out[...] = pick(src_v[...].reshape(2 * rows, tile))
        send_p()
        send_u()
        u_in[...] = jnp.zeros_like(u_in)
        p_in[...] = jnp.zeros_like(p_in)

    side = side_ref[...]

    loads[1].wait()
    b_re, b_im = basis_f[0], basis_f[1]
    top = jnp.concatenate([b_re, -b_im], axis=0)
    bottom = jnp.concatenate([b_im, b_re], axis=0)
    for i, m in enumerate((top, bottom)):
        hi, lo = halves(m)
        basis_w[: 2 * rank, i * tile : (i + 1) * tile] = hi
        basis_w[2 * rank :, i * tile : (i + 1) * tile] = lo
    picked = mm(jnp.concatenate(thirds(jnp.concatenate([b_re, b_im], axis=0)), axis=0), pick_w[...])
    n = 2 * rank
    picked = picked[:n] + picked[n : 2 * n] + picked[2 * n :]
    s_re, s_im = picked[:rank], picked[rank:]
    s_mat = jnp.concatenate([jnp.where(first, s_re, s_im), jnp.where(first, -s_im, s_re)], axis=0)
    s_hi, s_lo = halves(s_mat)
    s_w = jnp.concatenate([s_hi, s_lo], axis=1)
    loads[2].wait()

    @pl.loop(0, nt // 2)
    def _(t):
        at = pl.ds(pl.multiple_of(t * 2 * rank, 2 * rank), 2 * rank)
        re, im = coup_f[0, :, at], coup_f[1, :, at]
        re_r, im_r = pltpu.roll(re, rank, 1), pltpu.roll(im, rank, 1)
        for odd in range(2):
            c = 2 * t + odd
            if odd == 0:
                a = jnp.concatenate([jnp.where(first, re, -im_r), jnp.where(first, im, re_r)], axis=0)
            else:
                a = jnp.concatenate([jnp.where(first, re_r, -im), jnp.where(first, im_r, re)], axis=0)
            keep = jnp.logical_and(side + me != c, me != c).astype(F32)
            a = (a * keep).T
            hi, lo = halves(a)
            prod = mm(jnp.concatenate([hi, lo], axis=0), s_w)
            w = prod[:n, :n] + prod[n:, :n] + prod[:n, n:]
            w_hi, w_lo = halves(w)
            cx, cz = c // nz, c % nz
            out_at = pl.ds(pl.multiple_of(cx * n, n), n)
            wp[cz, out_at, :n] = w_hi
            wp[cz, out_at, n:] = w_lo
            wc[cz, out_at, :n] = hi
            wc[cz, out_at, n:] = lo

    for slot in range(2):
        for part in range(2):
            loads[3 + 2 * slot + part].wait()

            @pl.loop(0, tile // 32)
            def _(i):
                at = pl.ds(pl.multiple_of(i * 32, 32), 32)
                hi, lo = halves(near_f[slot, part, at, :])
                near_hi[slot, part, at, :] = hi
                near_lo[slot, part, at, :] = lo

    @pl.when(has_prev)
    def _():
        for i in range(3):
            pltpu.make_async_copy(u_in.at[i], u_in.at[i], u_recv.at[i]).wait()

    own = u_in[0].reshape(2 * rows, tile)
    beside = jnp.where(
        jnp.broadcast_to(side, (2 * rows, tile)) > 0,
        u_in[2].reshape(2 * rows, tile),
        u_in[1].reshape(2 * rows, tile),
    )
    sums = []
    lhs = [halves(own), halves(beside)]
    for part in range(2):
        total = None
        for slot in range(2):
            hi, lo = lhs[slot]
            both = mm(jnp.concatenate([hi, lo], axis=0), near_hi[slot, part])
            term = both[: 2 * rows] + both[2 * rows :] + mm(hi, near_lo[slot, part])
            total = term if total is None else total + term
        sums.append(total)
    n_re = sums[0][:rows] - sums[1][rows:] + src_v[0]
    n_im = sums[1][:rows] + sums[0][rows:] + src_v[1]
    u_new = jnp.concatenate([n_re, n_im], axis=0)
    ahead = pick(u_new)

    acc_p = jnp.zeros((2 * rows, 2 * n), F32)
    acc_c = jnp.zeros((2 * rows, 2 * n), F32)
    order = [int(outward(k, nz)) for k in range(nz)][::-1]
    for i, dz in enumerate(order):

        @pl.when(has_prev)
        def _():
            pltpu.make_async_copy(p_in.at[dz], p_in.at[dz], p_recv.at[dz]).wait()

        got = jnp.concatenate([p_in[dz, x] for x in range(nx)], axis=1)
        got = jnp.concatenate(halves(got), axis=0)
        cz = (my_z - dz + nz) % nz
        acc_p += mm(got, wp[cz])
        if i == nz - 1:
            fold = acc_p[:rows] + acc_p[rows:]
            p_new = ahead + fold[:, :n] + fold[:, n:]

            @pl.when(jnp.logical_and(has_prev, has_next))
            def _():
                p_out[...] = p_new
                send_p()

        acc_c += mm(got, wc[cz])
    fold = acc_c[:rows] + acc_c[rows:]
    coef = fold[:, :n] + fold[:, n:]
    c_hi, c_lo = halves(coef)
    lhs_c = jnp.concatenate(
        [jnp.concatenate([c_hi, c_hi], axis=1), jnp.concatenate([c_lo, c_lo], axis=1)], axis=0
    )
    far = mm(lhs_c, basis_w[...])
    far = far[:rows] + far[rows:]
    u_re = n_re + far[:, :tile]
    u_im = n_im + far[:, tile:]

    @pl.when(has_prev)
    def _():
        u_out[0] = u_re
        u_out[1] = u_im

    @pl.when(jnp.logical_and(has_prev, has_next))
    def _():
        send_u()

    part_sum = jnp.sum(u_re * u_re + u_im * u_im, axis=1, keepdims=True)
    diag = (
        lax.broadcasted_iota(jnp.int32, (rows, 128), 0)
        == lax.broadcasted_iota(jnp.int32, (rows, 128), 1)
    ).astype(F32)
    e_out[...] = jnp.sum(part_sum * diag, axis=0, keepdims=True)

    @pl.loop(1, nt)
    def _(k):
        rel = outward(k - 1, nt - 1) + 1
        pltpu.make_async_remote_copy(
            src_ref=e_out,
            dst_ref=e_in.at[rel - 1],
            send_sem=e_send,
            recv_sem=e_recv,
            device_id=(slab, (me + rel) % nt),
            device_id_type=MESH,
        ).start()

    pltpu.make_async_copy(e_in, e_in, e_recv).wait()
    total = e_out[...] + jnp.sum(e_in[...], axis=0)
    energy = jnp.sum(total * diag, axis=1, keepdims=True) / (2 * tile * nt)
    scale = 1.0 / jnp.sqrt(energy + small_eps)
    out_ref[0] = u_re * scale
    out_ref[1] = u_im * scale

    pltpu.make_async_copy(e_in, e_in, e_send).wait()

    @pl.when(has_next)
    def _():
        for i in range(3):
            pltpu.make_async_copy(u_out, u_out, u_send.at[i]).wait()
        pltpu.make_async_copy(p_in, p_in, p_send).wait()

    @pl.when(has_prev)
    def _():
        skel_copy.wait_send()


def solution(mesh):
    ns, nt = mesh.shape["slab"], mesh.shape["trace"]
    nz = 8 if nt % 8 == 0 else nt // 2
    nx = nt // nz

    def on_device(near_tiles, near_side, skeleton, far_coupling, far_basis, sources):
        rows, tile = sources.shape[2] * sources.shape[3], sources.shape[4]
        rank = skeleton.shape[2]
        any_space = pl.BlockSpec(memory_space=pl.ANY)
        vmem = pl.BlockSpec(memory_space=pltpu.VMEM)
        dma = pltpu.SemaphoreType.DMA
        result = pl.pallas_call(
            functools.partial(kernel, (ns, nt, nx, nz)),
            out_shape=jax.ShapeDtypeStruct((2, rows, tile), F32),
            in_specs=[any_space, vmem, vmem, any_space, any_space, any_space],
            out_specs=vmem,
            scratch_shapes=[
                pltpu.VMEM((2, 2, tile, tile), F32),
                pltpu.VMEM((2, 2, tile, tile), BF16),
                pltpu.VMEM((2, 2, tile, tile), BF16),
                pltpu.VMEM((2, rank, nt * rank), F32),
                pltpu.VMEM((2, rank, tile), F32),
                pltpu.VMEM((4 * rank, 2 * tile), BF16),
                pltpu.VMEM((2, rows, tile), F32),
                pltpu.VMEM((8, 2 * rank), jnp.int32),
                pltpu.VMEM((8, 2 * rank), jnp.int32),
                pltpu.VMEM((tile, 2 * rank), BF16),
                pltpu.VMEM((nz, nx * 2 * rank, 4 * rank), BF16),
                pltpu.VMEM((nz, nx * 2 * rank, 4 * rank), BF16),
                pltpu.VMEM((3, 2, rows, tile), F32),
                pltpu.VMEM((2, rows, tile), F32),
                pltpu.VMEM((nz, nx, rows, 2 * rank), F32),
                pltpu.VMEM((rows, 2 * rank), F32),
                pltpu.VMEM((nt - 1, 1, 128), F32),
                pltpu.VMEM((1, 128), F32),
                dma((7,)),
                dma((2,)),
                dma((3,)),
                dma((3,)),
                dma,
                dma((nz,)),
                dma,
                dma,
            ],
            compiler_params=pltpu.CompilerParams(collective_id=0, has_side_effects=True),
        )(
            near_tiles[0],
            near_side,
            skeleton[0],
            far_coupling[0],
            far_basis[0],
            sources[0].reshape(2, rows, tile),
        )
        return result.reshape(sources.shape)

    placed = (
        P("slab", None, None, None, "trace"),
        P("slab", "trace"),
        P("slab", "trace", None),
        P("slab", None, "trace", None),
        P("slab", None, None, "trace"),
        P("slab", None, None, None, "trace"),
    )
    return jax.shard_map(
        on_device,
        mesh=mesh,
        in_specs=placed,
        out_specs=P("slab", None, None, None, "trace"),
        check_vma=False,
    )
```

time: 860 us -> 103 us (0.12)
  the two profiles are of different devices: /device:TPU:24 before, /device:TPU:25 now
where the time goes in v1:
time: 103 us
  Pallas kernels  101 us (98%)
  local copies, waits for them, and re-layouts  1.54 us (1%)
    pallas_call x1, Pallas kernels, on_device(): pl.pallas_call(functools.partial(kernel, (ns, nt, nx, nz)), out_shape=jax...  101 us

profile of v1, /device:TPU:25, one launch (start us, length us, event | category | flops | bytes accessed | tf_op | source)
XLA Modules:
  0.0 103.2 jit_solution(7758104027482647411)
XLA Ops:
  0.7 101.0 %shard_map.64 = f32[2,16,768]{2,1,0:T(8,128)} custom-call(f32[2,2,768,768]{3,2,1,0:T(8,128)} %bitcast.8, s32[1,1]{1,0:T(1,128)S(6)} %copy.9.side_ref, s32[1,64]{1,0:T(1,128)} %bitcast.13, f32[2,64,2048]{2,1,0:T(8,128)} %bitcast.9, f32[2,64,768]{2,1,0:T(8,128)} %bitcast.11, f32[2,16,768]{2,1,0:T(8,128)} %bitcast.12), custom_call_target="tpu_custom_call" | custom-call | tf_op jit(solution)/shard_map/pallas_call | solution.py:365
  101.6 1.5 %copy.10 = f32[1,2,1,16,768]{4,3,2,1,0:T(8,128)} copy(f32[1,2,1,16,768]{4,3,2,1,0:T(8,128)} %bitcast.10) | data formatting | bytes 196608

commit v2 on v1

v2 whole, which is shorter than its diff:
```python
import functools

import jax
import jax.numpy as jnp
from jax import lax
from jax.experimental import pallas as pl
from jax.experimental.pallas import tpu as pltpu
from jax.sharding import PartitionSpec as P

MESH = pl.DeviceIdType.MESH
F32 = jnp.float32
BF16 = jnp.bfloat16
small_eps = 1e-06


def halves(x):
    hi = x.astype(BF16)
    lo = (x - hi.astype(F32)).astype(BF16)
    return hi, lo


def thirds(x):
    hi = x.astype(BF16)
    rest = x - hi.astype(F32)
    mid = rest.astype(BF16)
    lo = (rest - mid.astype(F32)).astype(BF16)
    return hi, mid, lo


def mm(a, b):
    return jnp.dot(a, b, preferred_element_type=F32)


def outward(k, n):
    return (n // 2 + ((k + 1) // 2) * (1 - 2 * (k % 2))) % n


def joined(x):
    hi = x.astype(BF16).astype(F32)
    return jnp.concatenate([hi, x - hi], axis=0).astype(BF16)


def kernel(
    sizes,
    near_hbm,
    side_ref,
    skel_ref,
    coup_hbm,
    basis_hbm,
    src_hbm,
    u_hbm,
    scale_ref,
    near_f,
    near_hi,
    near_lo,
    coup_f,
    basis_f,
    basis_in,
    basis_w,
    src_v,
    skel_out,
    skel_next,
    pick_w,
    wp,
    wc,
    n_in,
    n_out,
    c_in,
    c_out,
    p_in,
    p_out,
    e_in,
    e_out,
    u_v,
    w_sem,
    skel_sem,
    b_send,
    b_recv,
    n_send,
    n_recv,
    c_send,
    c_recv,
    p_send,
    p_recv,
    e_send,
    e_recv,
):
    ns, nt, nx, nz = sizes
    tile = src_v.shape[2]
    rows = src_v.shape[1]
    rank = skel_ref.shape[1]
    n = 2 * rank
    half = rows // 2
    slab = lax.axis_index("slab")
    me = lax.axis_index("trace")
    my_x, my_z = me // nz, me % nz
    has_next = slab < ns - 1
    has_prev = slab > 0
    from_far = slab > 1
    first = lax.broadcasted_iota(jnp.int32, (rank, n), 1) < rank

    basis_load = pltpu.make_async_copy(basis_hbm, basis_f, w_sem.at[0])
    coup_load = pltpu.make_async_copy(coup_hbm, coup_f, w_sem.at[1])
    src_load = pltpu.make_async_copy(src_hbm, src_v, w_sem.at[2])
    near_loads = [
        pltpu.make_async_copy(
            near_hbm.at[slot, part], near_f.at[slot, part], w_sem.at[3 + 2 * slot + part]
        )
        for slot in range(2)
        for part in range(2)
    ]
    for load in [src_load, coup_load, basis_load] + near_loads:
        load.start()

    spread = [
        (int(outward(k // nx, nz)), int(outward(k % nx, nx))) for k in range(nt)
    ]
    wrap_x = [lax.rem(my_x + dx, nx) * nz for dx in range(nx)]
    wrap_z = [lax.rem(my_z + dz, nz) for dz in range(nz)]

    def block_at(dz, dx):
        return wrap_x[dx] + wrap_z[dz]

    barrier = pltpu.get_barrier_semaphore()

    def greet(s, t):
        pl.semaphore_signal(barrier, inc=1, device_id=(s, t), device_id_type=MESH)

    @pl.when(has_prev)
    def _():
        for dz, dx in spread:
            greet(slab - 1, block_at(dz, dx))

    for dz, dx in spread[:-1]:
        greet(slab, block_at(dz, dx))

    @pl.when(has_next)
    def _():
        greet(slab + 1, me)

    twin = jnp.concatenate([skel_ref[...], skel_ref[...]], axis=1)
    skel_out[...] = jnp.broadcast_to(twin, skel_out.shape)
    side = side_ref[...]

    def choose(right, left):
        return jnp.where(jnp.broadcast_to(side, left.shape) > 0, right, left)

    def set_basis(i, b_re, b_im):
        top = jnp.concatenate([b_re, -b_im], axis=0)
        bottom = jnp.concatenate([b_im, b_re], axis=0)
        for j, m in enumerate((top, bottom)):
            hi, lo = halves(m)
            basis_w[i, :n, j * tile : (j + 1) * tile] = hi
            basis_w[i, n:, j * tile : (j + 1) * tile] = lo

    def far_part(i, coef):
        hi, lo = halves(coef)
        lhs = jnp.concatenate(
            [jnp.concatenate([hi, hi], axis=1), jnp.concatenate([lo, lo], axis=1)], axis=0
        )
        far = mm(lhs, basis_w[i])
        far = far[:rows] + far[rows:]
        return far[:, :tile], far[:, tile:]

    coup_load.wait()
    place = lax.broadcasted_iota(jnp.int32, (n, n), 1)

    @pl.loop(0, nt // 2, unroll=min(4, nt // 2))
    def _(t):
        at = pl.ds(pl.multiple_of(t * n, n), n)
        a = jnp.concatenate([coup_f[0, :, at], coup_f[1, :, at]], axis=0).T
        b = pltpu.roll(jnp.where(place < rank, a, -a), rank, 1)
        for odd in range(2):
            c = 2 * t + odd
            keep = jnp.logical_and(side + me != c, me != c).astype(F32)
            cx, cz = c // nz, c % nz
            for i, m in enumerate((a, b)):
                hi, lo = halves(m[odd * rank : (odd + 1) * rank] * keep)
                out_at = pl.ds(pl.multiple_of(cx * n + i * rank, rank), rank)
                wc[cz, out_at, :n] = hi
                wc[cz, out_at, n:] = lo

    basis_load.wait()
    set_basis(0, basis_f[0], basis_f[1])
    src_load.wait()

    pl.semaphore_wait(
        barrier, nt - 1 + nt * has_next.astype(jnp.int32) + has_prev.astype(jnp.int32)
    )

    skel_copy = pltpu.make_async_remote_copy(
        src_ref=skel_out,
        dst_ref=skel_next,
        send_sem=skel_sem.at[0],
        recv_sem=skel_sem.at[1],
        device_id=(slab - 1, me),
        device_id_type=MESH,
    )

    @pl.when(has_prev)
    def _():
        skel_copy.start()

    def send_three(src, dst, send, recv):
        for i, shift in enumerate((nt - 1, 1, 0)):
            pltpu.make_async_remote_copy(
                src_ref=src,
                dst_ref=dst.at[i],
                send_sem=send.at[i],
                recv_sem=recv.at[i],
                device_id=(slab + 1, (me + shift) % nt),
                device_id_type=MESH,
            ).start()

    def send_p(stream):
        for dz, dx in spread:
            pltpu.make_async_remote_copy(
                src_ref=p_out.at[stream],
                dst_ref=p_in.at[stream, dz, my_x],
                send_sem=p_send.at[stream],
                recv_sem=p_recv.at[stream, dz],
                device_id=(slab + 1, block_at(dz, dx)),
                device_id_type=MESH,
            ).start()

    def pick(x):
        parts = mm(jnp.concatenate(thirds(x), axis=0), pick_w[...])
        m = 2 * rows
        got = parts[:m] + parts[m : 2 * m] + parts[2 * m :]
        return jnp.where(first[:rows], got[:rows], got[rows:])

    @pl.when(slab == 0)
    def _():
        send_three(src_v, n_in, n_send, n_recv)
        n_in[...] = jnp.zeros_like(n_in)
        p_in[...] = jnp.zeros_like(p_in)

    @pl.when(jnp.logical_and(has_prev, has_next))
    def _():
        send_three(basis_f, basis_in, b_send, b_recv)

    @pl.when(has_next)
    def _():
        skel_copy.wait_recv()
        unknown = lax.broadcasted_iota(jnp.int32, (tile, n), 0)
        pick_w[...] = (unknown == skel_next[:1, :]).astype(BF16)

    @pl.when(jnp.logical_not(has_next))
    def _():
        pick_w[...] = jnp.zeros_like(pick_w)

    @pl.when(slab == 0)
    def _():
        p_first = pick(src_v[...].reshape(2 * rows, tile))
        for stream in range(2):
            p_out[stream] = p_first[stream * half : (stream + 1) * half]
            send_p(stream)

    for slot in range(2):
        for part in range(2):
            near_loads[2 * slot + part].wait()

            @pl.loop(0, tile // 32)
            def _(i):
                at = pl.ds(pl.multiple_of(i * 32, 32), 32)
                hi, lo = halves(near_f[slot, part, at, :])
                near_hi[slot, part, at, :] = hi
                near_lo[slot, part, at, :] = lo

    b_all = basis_f[...].reshape(n, tile)
    picked = mm(jnp.concatenate(thirds(b_all), axis=0), pick_w[...])
    picked = picked[:n] + picked[n : 2 * n] + picked[2 * n :]
    s_re, s_im = picked[:rank], picked[rank:]
    s_mat = jnp.concatenate([jnp.where(first, s_re, s_im), jnp.where(first, -s_im, s_re)], axis=0)
    s_w = jnp.concatenate(halves(s_mat), axis=1)
    s_w = jnp.concatenate([s_w, s_w], axis=0)

    @pl.loop(0, nz, unroll=2)
    def _(z):
        prod = mm(wc[z], s_w)
        hi, lo = halves(prod[:, :n] + prod[:, n:])
        wp[z, :, :n] = hi
        wp[z, :, n:] = lo

    def near(slot, x, m):
        hi, lo = halves(x)
        both = jnp.concatenate([hi, lo], axis=0)
        sums = []
        for part in range(2):
            prod = mm(both, near_hi[slot, part])
            sums.append(prod[: 2 * m] + prod[2 * m :] + mm(hi, near_lo[slot, part]))
        return sums[0][:m] - sums[1][m:], sums[1][:m] + sums[0][m:]

    @pl.when(from_far)
    def _():
        for i in range(3):
            pltpu.make_async_copy(basis_in.at[i], basis_in.at[i], b_recv.at[i]).wait()
        set_basis(1, *near(0, basis_in[2].reshape(n, tile), rank))
        beside = jnp.where(
            jnp.broadcast_to(side, (n, tile)) > 0,
            basis_in[0].reshape(n, tile),
            basis_in[1].reshape(n, tile),
        )
        set_basis(2, *near(1, beside, rank))

    @pl.when(has_prev)
    def _():
        for i in range(3):
            pltpu.make_async_copy(n_in.at[i], n_in.at[i], n_recv.at[i]).wait()

    own_re, own_im = near(0, n_in[2].reshape(2 * rows, tile), rows)
    next_re, next_im = near(1, choose(n_in[0], n_in[1]).reshape(2 * rows, tile), rows)
    n_out[0] = own_re + next_re + src_v[0]
    n_out[1] = own_im + next_im + src_v[1]

    order = [int(outward(k, nz)) for k in range(nz)][::-1]
    early = order[: nz // 2 + 1]
    late = order[nz // 2 + 1 :]

    def wait_p(stream, group):
        @pl.when(has_prev)
        def _():
            for dz in group:
                pltpu.make_async_copy(
                    p_in.at[stream, dz], p_in.at[stream, dz], p_recv.at[stream, dz]
                ).wait()

    def p_lhs(stream, dz):
        return joined(jnp.concatenate([p_in[stream, dz, x] for x in range(nx)], axis=1))

    def times(w, stream, group):
        total = None
        for dz in group:
            term = mm(p_lhs(stream, dz), w[(my_z - dz + nz) % nz])
            total = term if total is None else total + term
        return total

    def fold(acc):
        acc = acc[:half] + acc[half:]
        return acc[:, :n] + acc[:, n:]

    wait_p(0, early)
    p_acc = times(wp, 0, early)
    c_acc = times(wc, 0, early)

    @pl.when(from_far)
    def _():
        for i in range(3):
            pltpu.make_async_copy(c_in.at[i], c_in.at[i], c_recv.at[i]).wait()
        f_re, f_im = far_part(1, c_in[2])
        g_re, g_im = far_part(2, choose(c_in[0], c_in[1]))
        n_out[0] += f_re + g_re
        n_out[1] += f_im + g_im

    @pl.when(jnp.logical_and(has_prev, has_next))
    def _():
        send_three(n_out, n_in, n_send, n_recv)

    n_re, n_im = n_out[0], n_out[1]
    ahead = pick(jnp.concatenate([n_re, n_im], axis=0))

    coefs = []
    for stream in range(2):
        if stream == 1:
            wait_p(1, early)
            p_acc = times(wp, 1, early)
            c_acc = times(wc, 1, early)
        wait_p(stream, late)
        p_new = ahead[stream * half : (stream + 1) * half] + fold(p_acc + times(wp, stream, late))
        if stream == 1:
            coefs.append(fold(c_acc + times(wc, stream, late)))

        @pl.when(jnp.logical_and(has_prev, has_next))
        def _():
            p_out[stream] = p_new
            if stream == 1:
                c_out[...] = jnp.concatenate(coefs, axis=0)
                send_three(c_out, c_in, c_send, c_recv)
            send_p(stream)

        if stream == 0:
            coefs.append(fold(c_acc + times(wc, stream, late)))
    coef = jnp.concatenate(coefs, axis=0)

    f_re, f_im = far_part(0, coef)
    u_re = n_re + f_re
    u_im = n_im + f_im

    part_sum = jnp.sum(u_re * u_re + u_im * u_im, axis=1, keepdims=True)
    diag = (
        lax.broadcasted_iota(jnp.int32, (rows, 128), 0)
        == lax.broadcasted_iota(jnp.int32, (rows, 128), 1)
    ).astype(F32)
    e_out[...] = jnp.sum(part_sum * diag, axis=0, keepdims=True)

    for k, (dz, dx) in enumerate(spread[:-1]):
        pltpu.make_async_remote_copy(
            src_ref=e_out,
            dst_ref=e_in.at[k],
            send_sem=e_send,
            recv_sem=e_recv,
            device_id=(slab, block_at(dz, dx)),
            device_id_type=MESH,
        ).start()

    u_v[0] = u_re
    u_v[1] = u_im
    u_store = pltpu.make_async_copy(u_v, u_hbm, w_sem.at[7])
    u_store.start()

    pltpu.make_async_copy(e_in, e_in, e_recv).wait()
    total = e_out[...] + jnp.sum(e_in[...], axis=0)
    energy = jnp.sum(total * diag, axis=1, keepdims=True) / (2 * tile * nt)
    scale_ref[...] = jnp.broadcast_to(1.0 / jnp.sqrt(energy + small_eps), scale_ref.shape)

    u_store.wait()
    pltpu.make_async_copy(e_in, e_in, e_send).wait()

    @pl.when(has_next)
    def _():
        for i in range(3):
            pltpu.make_async_copy(n_out, n_out, n_send.at[i]).wait()
        for stream in range(2):
            pltpu.make_async_copy(p_in.at[stream], p_in.at[stream], p_send.at[stream]).wait()

    @pl.when(jnp.logical_and(has_prev, has_next))
    def _():
        for i in range(3):
            pltpu.make_async_copy(basis_f, basis_f, b_send.at[i]).wait()
            pltpu.make_async_copy(c_out, c_out, c_send.at[i]).wait()

    @pl.when(has_prev)
    def _():
        skel_copy.wait_send()


def solution(mesh):
    ns, nt = mesh.shape["slab"], mesh.shape["trace"]
    nz = 8 if nt % 8 == 0 else nt
    nx = nt // nz

    def on_device(near_tiles, near_side, skeleton, far_coupling, far_basis, sources):
        rows, tile = sources.shape[2] * sources.shape[3], sources.shape[4]
        rank = skeleton.shape[2]
        any_space = pl.BlockSpec(memory_space=pl.ANY)
        vmem = pl.BlockSpec(memory_space=pltpu.VMEM)
        dma = pltpu.SemaphoreType.DMA
        u, scale = pl.pallas_call(
            functools.partial(kernel, (ns, nt, nx, nz)),
            out_shape=(
                jax.ShapeDtypeStruct((2, rows, tile), F32),
                jax.ShapeDtypeStruct((rows, tile), F32),
            ),
            in_specs=[any_space, vmem, vmem, any_space, any_space, any_space],
            out_specs=(any_space, vmem),
            scratch_shapes=[
                pltpu.VMEM((2, 2, tile, tile), F32),
                pltpu.VMEM((2, 2, tile, tile), BF16),
                pltpu.VMEM((2, 2, tile, tile), BF16),
                pltpu.VMEM((2, rank, nt * rank), F32),
                pltpu.VMEM((2, rank, tile), F32),
                pltpu.VMEM((3, 2, rank, tile), F32),
                pltpu.VMEM((3, 4 * rank, 2 * tile), BF16),
                pltpu.VMEM((2, rows, tile), F32),
                pltpu.VMEM((8, 2 * rank), jnp.int32),
                pltpu.VMEM((8, 2 * rank), jnp.int32),
                pltpu.VMEM((tile, 2 * rank), BF16),
                pltpu.VMEM((nz, nx * 2 * rank, 4 * rank), BF16),
                pltpu.VMEM((nz, nx * 2 * rank, 4 * rank), BF16),
                pltpu.VMEM((3, 2, rows, tile), F32),
                pltpu.VMEM((2, rows, tile), F32),
                pltpu.VMEM((3, rows, 2 * rank), F32),
                pltpu.VMEM((rows, 2 * rank), F32),
                pltpu.VMEM((2, nz, nx, rows // 2, 2 * rank), F32),
                pltpu.VMEM((2, rows // 2, 2 * rank), F32),
                pltpu.VMEM((nt - 1, 1, 128), F32),
                pltpu.VMEM((1, 128), F32),
                pltpu.VMEM((2, rows, tile), F32),
                dma((8,)),
                dma((2,)),
                dma((3,)),
                dma((3,)),
                dma((3,)),
                dma((3,)),
                dma((3,)),
                dma((3,)),
                dma((2,)),
                dma((2, nz)),
                dma,
                dma,
            ],
            compiler_params=pltpu.CompilerParams(collective_id=0, has_side_effects=True),
        )(
            near_tiles[0],
            near_side,
            skeleton[0],
            far_coupling[0],
            far_basis[0],
            sources[0].reshape(2, rows, tile),
        )
        return (u * scale[None]).reshape(sources.shape)

    placed = (
        P("slab", None, None, None, "trace"),
        P("slab", "trace"),
        P("slab", "trace", None),
        P("slab", None, "trace", None),
        P("slab", None, None, "trace"),
        P("slab", None, None, None, "trace"),
    )
    return jax.shard_map(
        on_device,
        mesh=mesh,
        in_specs=placed,
        out_specs=P("slab", None, None, None, "trace"),
        check_vma=False,
    )
```

time: 103 us -> 92.6 us (0.90)
  Pallas kernels: 101 us -> 90.3 us
  other arithmetic: 0 us -> 1.55 us
  local copies, waits for them, and re-layouts: 1.54 us -> 0 us
    pallas_call x1, Pallas kernels: 101 us -> 90.3 us  [on_device(): pl.pallas_call(functools.partial(kernel, (ns, nt, nx, nz)), out_shape=(ja...]
    reshape x0 -> x1, other arithmetic: none -> 1.55 us  [on_device(): return (u * scale[None]).reshape(sources.shape)]
    unnamed x1 -> x0, local copies, waits for them, and re-layouts: 1.54 us -> none
where the time goes in v2:
time: 92.6 us; the launch traced here: 92.5 us
  Pallas kernels  90.3 us (98%)
  other arithmetic  1.55 us (2%)
    pallas_call x1, Pallas kernels, on_device(): pl.pallas_call(functools.partial(kernel, (ns, nt, nx, nz)), out_shape=(ja...  90.3 us

profile of v2, /device:TPU:25, one launch (start us, length us, event | category | flops | bytes accessed | tf_op | source)
XLA Modules:
  0.0 92.5 jit_solution(4327594580668324752)
XLA Ops:
  0.7 90.3 %shard_map.64 = (f32[2,16,768]{2,1,0:T(8,128)}, f32[16,768]{1,0:T(8,128)}) custom-call(f32[2,2,768,768]{3,2,1,0:T(8,128)} %bitcast.9, s32[1,1]{1,0:T(1,128)S(6)} %copy.8.side_ref, s32[1,64]{1,0:T(1,128)} %bitcast.13, f32[2,64,2048]{2,1,0:T(8,128)} %bitcast.10, f32[2,64,768]{2,1,0:T(8,128)} %bitcast.11, f32[2,16,768]{2,1,0:T(8,128)} %bitcast.12), custom_call_target="tpu_custom_call" | custom-call | tf_op jit(solution)/shard_map/pallas_call | solution.py:448
  90.9 1.5 %multiply_bitcast_fusion = f32[1,2,1,16,768]{4,3,2,1,0:T(8,128)} fusion(f32[2,16,768]{2,1,0:T(8,128)} %get-tuple-element.7, f32[16,768]{1,0:T(8,128)} %get-tuple-element.8), kind=kLoop, calls=%fused_computation | loop fusion | flops 24576 | bytes 245760 | tf_op jit(solution)/shard_map/reshape | solution.py:501

commit v3 on v2

--- a/solution.py
+++ b/solution.py
@@ -55,31 +55,27 @@
     near_lo,
     coup_f,
     basis_f,
-    basis_in,
     basis_w,
+    nsel,
+    a_v,
+    acc_v,
     src_v,
     skel_out,
     skel_next,
     pick_w,
     wp,
     wc,
-    n_in,
-    n_out,
-    c_in,
-    c_out,
+    u_in,
+    u_out,
+    n_v,
     p_in,
     p_out,
     e_in,
     e_out,
-    u_v,
     w_sem,
     skel_sem,
-    b_send,
-    b_recv,
-    n_send,
-    n_recv,
-    c_send,
-    c_recv,
+    u_send,
+    u_recv,
     p_send,
     p_recv,
     e_send,
@@ -145,20 +141,20 @@
     def choose(right, left):
         return jnp.where(jnp.broadcast_to(side, left.shape) > 0, right, left)
 
-    def set_basis(i, b_re, b_im):
+    def set_basis(b_re, b_im):
         top = jnp.concatenate([b_re, -b_im], axis=0)
         bottom = jnp.concatenate([b_im, b_re], axis=0)
         for j, m in enumerate((top, bottom)):
             hi, lo = halves(m)
-            basis_w[i, :n, j * tile : (j + 1) * tile] = hi
-            basis_w[i, n:, j * tile : (j + 1) * tile] = lo
-
-    def far_part(i, coef):
+            basis_w[:n, j * tile : (j + 1) * tile] = hi
+            basis_w[n:, j * tile : (j + 1) * tile] = lo
+
+    def far_part(coef):
         hi, lo = halves(coef)
         lhs = jnp.concatenate(
             [jnp.concatenate([hi, hi], axis=1), jnp.concatenate([lo, lo], axis=1)], axis=0
         )
-        far = mm(lhs, basis_w[i])
+        far = mm(lhs, basis_w[...])
         far = far[:rows] + far[rows:]
         return far[:, :tile], far[:, tile:]
 
@@ -181,7 +177,7 @@
                 wc[cz, out_at, n:] = lo
 
     basis_load.wait()
-    set_basis(0, basis_f[0], basis_f[1])
+    set_basis(basis_f[0], basis_f[1])
     src_load.wait()
 
     pl.semaphore_wait(
@@ -231,13 +227,9 @@
 
     @pl.when(slab == 0)
     def _():
-        send_three(src_v, n_in, n_send, n_recv)
-        n_in[...] = jnp.zeros_like(n_in)
+        send_three(src_v, u_in, u_send, u_recv)
+        u_in[...] = jnp.zeros_like(u_in)
         p_in[...] = jnp.zeros_like(p_in)
-
-    @pl.when(jnp.logical_and(has_prev, has_next))
-    def _():
-        send_three(basis_f, basis_in, b_send, b_recv)
 
     @pl.when(has_next)
     def _():
@@ -282,36 +274,43 @@
         wp[z, :, :n] = hi
         wp[z, :, n:] = lo
 
-    def near(slot, x, m):
-        hi, lo = halves(x)
-        both = jnp.concatenate([hi, lo], axis=0)
-        sums = []
-        for part in range(2):
-            prod = mm(both, near_hi[slot, part])
-            sums.append(prod[: 2 * m] + prod[2 * m :] + mm(hi, near_lo[slot, part]))
-        return sums[0][:m] - sums[1][m:], sums[1][:m] + sums[0][m:]
-
     @pl.when(from_far)
     def _():
+        in_first = lax.broadcasted_iota(jnp.int32, (tile, n), 1) < rank
+        for slot in range(2):
+            for i, w in enumerate((near_hi, near_lo)):
+                re, im = mm(w[slot, 0], pick_w[...]), mm(w[slot, 1], pick_w[...])
+                nsel[slot, :, i * n : (i + 1) * n] = jnp.where(in_first, re, im).astype(BF16)
+        a_v[...] = pick(src_v[...].reshape(2 * rows, tile))
+
+    def wait_u():
         for i in range(3):
-            pltpu.make_async_copy(basis_in.at[i], basis_in.at[i], b_recv.at[i]).wait()
-        set_basis(1, *near(0, basis_in[2].reshape(n, tile), rank))
-        beside = jnp.where(
-            jnp.broadcast_to(side, (n, tile)) > 0,
-            basis_in[0].reshape(n, tile),
-            basis_in[1].reshape(n, tile),
-        )
-        set_basis(2, *near(1, beside, rank))
-
-    @pl.when(has_prev)
-    def _():
-        for i in range(3):
-            pltpu.make_async_copy(n_in.at[i], n_in.at[i], n_recv.at[i]).wait()
-
-    own_re, own_im = near(0, n_in[2].reshape(2 * rows, tile), rows)
-    next_re, next_im = near(1, choose(n_in[0], n_in[1]).reshape(2 * rows, tile), rows)
-    n_out[0] = own_re + next_re + src_v[0]
-    n_out[1] = own_im + next_im + src_v[1]
+            pltpu.make_async_copy(u_in.at[i], u_in.at[i], u_recv.at[i]).wait()
+
+    def incoming(slot):
+        x = u_in[2] if slot == 0 else choose(u_in[0], u_in[1])
+        return halves(x.reshape(2 * rows, tile))
+
+    def near():
+        sums = [None, None]
+        for slot in range(2):
+            hi, lo = incoming(slot)
+            both = jnp.concatenate([hi, lo], axis=0)
+            for part in range(2):
+                prod = mm(both, near_hi[slot, part])
+                term = prod[: 2 * rows] + prod[2 * rows :] + mm(hi, near_lo[slot, part])
+                sums[part] = term if slot == 0 else sums[part] + term
+        n_v[0] = sums[0][:rows] - sums[1][rows:] + src_v[0]
+        n_v[1] = sums[1][:rows] + sums[0][rows:] + src_v[1]
+
+    @pl.when(jnp.logical_not(from_far))
+    def _():
+        @pl.when(has_prev)
+        def _():
+            wait_u()
+
+        near()
+        a_v[...] = pick(n_v[...].reshape(2 * rows, tile))
 
     order = [int(outward(k, nz)) for k in range(nz)][::-1]
     early = order[: nz // 2 + 1]
@@ -339,52 +338,63 @@
         acc = acc[:half] + acc[half:]
         return acc[:, :n] + acc[:, n:]
 
-    wait_p(0, early)
-    p_acc = times(wp, 0, early)
-    c_acc = times(wc, 0, early)
+    sends_on = jnp.logical_and(has_prev, has_next)
+
+    def first_part(stream):
+        wait_p(stream, early)
+
+        @pl.when(sends_on)
+        def _():
+            acc_v[...] = times(wp, stream, early)
+
+    def last_part(stream):
+        @pl.when(sends_on)
+        def _():
+            p_out[stream] = a_v[stream * half : (stream + 1) * half] + fold(
+                acc_v[...] + times(wp, stream, late)
+            )
+            send_p(stream)
+
+    first_part(0)
+    c_first = times(wc, 0, early)
 
     @pl.when(from_far)
     def _():
-        for i in range(3):
-            pltpu.make_async_copy(c_in.at[i], c_in.at[i], c_recv.at[i]).wait()
-        f_re, f_im = far_part(1, c_in[2])
-        g_re, g_im = far_part(2, choose(c_in[0], c_in[1]))
-        n_out[0] += f_re + g_re
-        n_out[1] += f_im + g_im
-
-    @pl.when(jnp.logical_and(has_prev, has_next))
-    def _():
-        send_three(n_out, n_in, n_send, n_recv)
-
-    n_re, n_im = n_out[0], n_out[1]
-    ahead = pick(jnp.concatenate([n_re, n_im], axis=0))
-
-    coefs = []
-    for stream in range(2):
-        if stream == 1:
-            wait_p(1, early)
-            p_acc = times(wp, 1, early)
-            c_acc = times(wc, 1, early)
-        wait_p(stream, late)
-        p_new = ahead[stream * half : (stream + 1) * half] + fold(p_acc + times(wp, stream, late))
-        if stream == 1:
-            coefs.append(fold(c_acc + times(wc, stream, late)))
-
-        @pl.when(jnp.logical_and(has_prev, has_next))
+        wait_u()
+
+        @pl.when(has_next)
         def _():
-            p_out[stream] = p_new
-            if stream == 1:
-                c_out[...] = jnp.concatenate(coefs, axis=0)
-                send_three(c_out, c_in, c_send, c_recv)
-            send_p(stream)
-
-        if stream == 0:
-            coefs.append(fold(c_acc + times(wc, stream, late)))
-    coef = jnp.concatenate(coefs, axis=0)
-
-    f_re, f_im = far_part(0, coef)
-    u_re = n_re + f_re
-    u_im = n_im + f_im
+            total = None
+            for slot in range(2):
+                term = mm(jnp.concatenate(incoming(slot), axis=0), nsel[slot])
+                total = term if total is None else total + term
+            total = total[: 2 * rows] + total[2 * rows :]
+            total = total[:, :n] + total[:, n:]
+            turned = pltpu.roll(total[rows:], rank, 1)
+            a_v[...] += total[:rows] + jnp.where(first[:rows], -turned, turned)
+
+    wait_p(0, late)
+    last_part(0)
+    first_part(1)
+    wait_p(1, late)
+    last_part(1)
+
+    @pl.when(from_far)
+    def _():
+        near()
+
+    coef = jnp.concatenate(
+        [fold(c_first + times(wc, 0, late)), fold(times(wc, 1, order))], axis=0
+    )
+    f_re, f_im = far_part(coef)
+    u_re = n_v[0] + f_re
+    u_im = n_v[1] + f_im
+    u_out[0] = u_re
+    u_out[1] = u_im
+
+    @pl.when(sends_on)
+    def _():
+        send_three(u_out, u_in, u_send, u_recv)
 
     part_sum = jnp.sum(u_re * u_re + u_im * u_im, axis=1, keepdims=True)
     diag = (
@@ -403,9 +413,7 @@
             device_id_type=MESH,
         ).start()
 
-    u_v[0] = u_re
-    u_v[1] = u_im
-    u_store = pltpu.make_async_copy(u_v, u_hbm, w_sem.at[7])
+    u_store = pltpu.make_async_copy(u_out, u_hbm, w_sem.at[7])
     u_store.start()
 
     pltpu.make_async_copy(e_in, e_in, e_recv).wait()
@@ -419,15 +427,9 @@
     @pl.when(has_next)
     def _():
         for i in range(3):
-            pltpu.make_async_copy(n_out, n_out, n_send.at[i]).wait()
+            pltpu.make_async_copy(u_out, u_out, u_send.at[i]).wait()
         for stream in range(2):
             pltpu.make_async_copy(p_in.at[stream], p_in.at[stream], p_send.at[stream]).wait()
-
-    @pl.when(jnp.logical_and(has_prev, has_next))
-    def _():
-        for i in range(3):
-            pltpu.make_async_copy(basis_f, basis_f, b_send.at[i]).wait()
-            pltpu.make_async_copy(c_out, c_out, c_send.at[i]).wait()
 
     @pl.when(has_prev)
     def _():
@@ -459,8 +461,10 @@
                 pltpu.VMEM((2, 2, tile, tile), BF16),
                 pltpu.VMEM((2, rank, nt * rank), F32),
                 pltpu.VMEM((2, rank, tile), F32),
-                pltpu.VMEM((3, 2, rank, tile), F32),
-                pltpu.VMEM((3, 4 * rank, 2 * tile), BF16),
+                pltpu.VMEM((4 * rank, 2 * tile), BF16),
+                pltpu.VMEM((2, tile, 4 * rank), BF16),
+                pltpu.VMEM((rows, 2 * rank), F32),
+                pltpu.VMEM((rows, 4 * rank), F32),
                 pltpu.VMEM((2, rows, tile), F32),
                 pltpu.VMEM((8, 2 * rank), jnp.int32),
                 pltpu.VMEM((8, 2 * rank), jnp.int32),
@@ -469,19 +473,13 @@
                 pltpu.VMEM((nz, nx * 2 * rank, 4 * rank), BF16),
                 pltpu.VMEM((3, 2, rows, tile), F32),
                 pltpu.VMEM((2, rows, tile), F32),
-                pltpu.VMEM((3, rows, 2 * rank), F32),
-                pltpu.VMEM((rows, 2 * rank), F32),
+                pltpu.VMEM((2, rows, tile), F32),
                 pltpu.VMEM((2, nz, nx, rows // 2, 2 * rank), F32),
                 pltpu.VMEM((2, rows // 2, 2 * rank), F32),
                 pltpu.VMEM((nt - 1, 1, 128), F32),
                 pltpu.VMEM((1, 128), F32),
-                pltpu.VMEM((2, rows, tile), F32),
                 dma((8,)),
                 dma((2,)),
-                dma((3,)),
-                dma((3,)),
-                dma((3,)),
-                dma((3,)),
                 dma((3,)),
                 dma((3,)),
                 dma((2,)),

time: 92.6 us -> 83.3 us (0.90)
  Pallas kernels: 90.3 us -> 81 us
    pallas_call x1, Pallas kernels: 90.3 us -> 81 us  [on_device(): pl.pallas_call(functools.partial(kernel, (ns, nt, nx, nz)), out_shape=(ja...]
where the time goes in v3:
time: 83.3 us; the launch traced here: 83.2 us
  Pallas kernels  81 us (97%)
  other arithmetic  1.55 us (2%)
    pallas_call x1, Pallas kernels, on_device(): pl.pallas_call(functools.partial(kernel, (ns, nt, nx, nz)), out_shape=(ja...  81 us

profile of v3, /device:TPU:25, one launch (start us, length us, event | category | flops | bytes accessed | tf_op | source)
XLA Modules:
  0.0 83.2 jit_solution(8597572164372093550)
XLA Ops:
  0.7 81.0 %shard_map.64 = (f32[2,16,768]{2,1,0:T(8,128)}, f32[16,768]{1,0:T(8,128)}) custom-call(f32[2,2,768,768]{3,2,1,0:T(8,128)} %bitcast.9, s32[1,1]{1,0:T(1,128)S(6)} %copy.8.side_ref, s32[1,64]{1,0:T(1,128)} %bitcast.13, f32[2,64,2048]{2,1,0:T(8,128)} %bitcast.10, f32[2,64,768]{2,1,0:T(8,128)} %bitcast.11, f32[2,16,768]{2,1,0:T(8,128)} %bitcast.12), custom_call_target="tpu_custom_call" | custom-call | tf_op jit(solution)/shard_map/pallas_call | solution.py:450
  81.6 1.5 %multiply_bitcast_fusion = f32[1,2,1,16,768]{4,3,2,1,0:T(8,128)} fusion(f32[2,16,768]{2,1,0:T(8,128)} %get-tuple-element.7, f32[16,768]{1,0:T(8,128)} %get-tuple-element.8), kind=kLoop, calls=%fused_computation | loop fusion | flops 24576 | bytes 245760 | tf_op jit(solution)/shard_map/reshape | solution.py:499

commit v4 on v3

--- a/solution.py
+++ b/solution.py
@@ -11,6 +11,7 @@
 F32 = jnp.float32
 BF16 = jnp.bfloat16
 small_eps = 1e-06
+pieces = 2
 
 
 def halves(x):
@@ -197,11 +198,11 @@
     def _():
         skel_copy.start()
 
-    def send_three(src, dst, send, recv):
+    def send_three(src, dst, send, recv, cols):
         for i, shift in enumerate((nt - 1, 1, 0)):
             pltpu.make_async_remote_copy(
                 src_ref=src,
-                dst_ref=dst.at[i],
+                dst_ref=dst.at[i, :, :, cols],
                 send_sem=send.at[i],
                 recv_sem=recv.at[i],
                 device_id=(slab + 1, (me + shift) % nt),
@@ -227,7 +228,10 @@
 
     @pl.when(slab == 0)
     def _():
-        send_three(src_v, u_in, u_send, u_recv)
+        for piece in range(pieces):
+            cols = slice(piece * tile // pieces, (piece + 1) * tile // pieces)
+            send_three(src_v.at[:, :, cols], u_in, u_send.at[piece], u_recv.at[piece], cols)
+
         u_in[...] = jnp.zeros_like(u_in)
         p_in[...] = jnp.zeros_like(p_in)
 
@@ -284,24 +288,27 @@
         a_v[...] = pick(src_v[...].reshape(2 * rows, tile))
 
     def wait_u():
-        for i in range(3):
-            pltpu.make_async_copy(u_in.at[i], u_in.at[i], u_recv.at[i]).wait()
+        for piece in range(pieces):
+            cols = slice(piece * tile // pieces, (piece + 1) * tile // pieces)
+            for i in range(3):
+                part = u_in.at[i, :, :, cols]
+                pltpu.make_async_copy(part, part, u_recv.at[piece, i]).wait()
 
     def incoming(slot):
         x = u_in[2] if slot == 0 else choose(u_in[0], u_in[1])
         return halves(x.reshape(2 * rows, tile))
 
-    def near():
+    def near(cols):
         sums = [None, None]
         for slot in range(2):
             hi, lo = incoming(slot)
             both = jnp.concatenate([hi, lo], axis=0)
             for part in range(2):
-                prod = mm(both, near_hi[slot, part])
-                term = prod[: 2 * rows] + prod[2 * rows :] + mm(hi, near_lo[slot, part])
+                prod = mm(both, near_hi[slot, part, :, cols])
+                term = prod[: 2 * rows] + prod[2 * rows :] + mm(hi, near_lo[slot, part, :, cols])
                 sums[part] = term if slot == 0 else sums[part] + term
-        n_v[0] = sums[0][:rows] - sums[1][rows:] + src_v[0]
-        n_v[1] = sums[1][:rows] + sums[0][rows:] + src_v[1]
+        n_v[0, :, cols] = sums[0][:rows] - sums[1][rows:] + src_v[0, :, cols]
+        n_v[1, :, cols] = sums[1][:rows] + sums[0][rows:] + src_v[1, :, cols]
 
     @pl.when(jnp.logical_not(from_far))
     def _():
@@ -309,7 +316,7 @@
         def _():
             wait_u()
 
-        near()
+        near(slice(0, tile))
         a_v[...] = pick(n_v[...].reshape(2 * rows, tile))
 
     order = [int(outward(k, nz)) for k in range(nz)][::-1]
@@ -340,23 +347,30 @@
 
     sends_on = jnp.logical_and(has_prev, has_next)
 
-    def first_part(stream):
-        wait_p(stream, early)
-
+    def far_ahead(stream, group, start):
         @pl.when(sends_on)
         def _():
-            acc_v[...] = times(wp, stream, early)
-
-    def last_part(stream):
-        @pl.when(sends_on)
-        def _():
-            p_out[stream] = a_v[stream * half : (stream + 1) * half] + fold(
-                acc_v[...] + times(wp, stream, late)
-            )
-            send_p(stream)
-
-    first_part(0)
+            term = times(wp, stream, group)
+            acc_v[stream] = term if start else acc_v[stream] + term
+
+    def emit(stream):
+        p_out[stream] = a_v[stream * half : (stream + 1) * half] + fold(acc_v[stream])
+        send_p(stream)
+
+    wait_p(0, early)
+    far_ahead(0, early, True)
     c_first = times(wc, 0, early)
+    wait_p(0, late)
+    far_ahead(0, late, False)
+
+    @pl.when(slab == 1)
+    def _():
+        emit(0)
+
+    c_first = fold(c_first + times(wc, 0, late))
+    wait_p(1, early)
+    far_ahead(1, early, True)
+    c_second = times(wc, 1, early)
 
     @pl.when(from_far)
     def _():
@@ -372,29 +386,33 @@
             total = total[:, :n] + total[:, n:]
             turned = pltpu.roll(total[rows:], rank, 1)
             a_v[...] += total[:rows] + jnp.where(first[:rows], -turned, turned)
-
-    wait_p(0, late)
-    last_part(0)
-    first_part(1)
+            emit(0)
+
     wait_p(1, late)
-    last_part(1)
-
-    @pl.when(from_far)
-    def _():
-        near()
-
-    coef = jnp.concatenate(
-        [fold(c_first + times(wc, 0, late)), fold(times(wc, 1, order))], axis=0
-    )
+    far_ahead(1, late, False)
+
+    @pl.when(sends_on)
+    def _():
+        emit(1)
+
+    coef = jnp.concatenate([c_first, fold(c_second + times(wc, 1, late))], axis=0)
     f_re, f_im = far_part(coef)
-    u_re = n_v[0] + f_re
-    u_im = n_v[1] + f_im
-    u_out[0] = u_re
-    u_out[1] = u_im
-
-    @pl.when(sends_on)
-    def _():
-        send_three(u_out, u_in, u_send, u_recv)
+    u_out[0] = f_re
+    u_out[1] = f_im
+    for piece in range(pieces):
+        cols = slice(piece * tile // pieces, (piece + 1) * tile // pieces)
+
+        @pl.when(from_far)
+        def _():
+            near(cols)
+
+        u_out[:, :, cols] += n_v[:, :, cols]
+
+        @pl.when(sends_on)
+        def _():
+            send_three(u_out.at[:, :, cols], u_in, u_send.at[piece], u_recv.at[piece], cols)
+
+    u_re, u_im = u_out[0], u_out[1]
 
     part_sum = jnp.sum(u_re * u_re + u_im * u_im, axis=1, keepdims=True)
     diag = (
@@ -426,8 +444,10 @@
 
     @pl.when(has_next)
     def _():
-        for i in range(3):
-            pltpu.make_async_copy(u_out, u_out, u_send.at[i]).wait()
+        for piece in range(pieces):
+            part = u_out.at[:, :, : tile // pieces]
+            for i in range(3):
+                pltpu.make_async_copy(part, part, u_send.at[piece, i]).wait()
         for stream in range(2):
             pltpu.make_async_copy(p_in.at[stream], p_in.at[stream], p_send.at[stream]).wait()
 
@@ -464,7 +484,7 @@
                 pltpu.VMEM((4 * rank, 2 * tile), BF16),
                 pltpu.VMEM((2, tile, 4 * rank), BF16),
                 pltpu.VMEM((rows, 2 * rank), F32),
-                pltpu.VMEM((rows, 4 * rank), F32),
+                pltpu.VMEM((2, rows, 4 * rank), F32),
                 pltpu.VMEM((2, rows, tile), F32),
                 pltpu.VMEM((8, 2 * rank), jnp.int32),
                 pltpu.VMEM((8, 2 * rank), jnp.int32),
@@ -480,8 +500,8 @@
                 pltpu.VMEM((1, 128), F32),
                 dma((8,)),
                 dma((2,)),
-                dma((3,)),
-                dma((3,)),
+                dma((pieces, 3)),
+                dma((pieces, 3)),
                 dma((2,)),
                 dma((2, nz)),
                 dma,

time: 83.3 us -> 79.5 us (0.954)
  Pallas kernels: 81 us -> 77.1 us
    pallas_call x1, Pallas kernels: 81 us -> 77.1 us  [on_device(): pl.pallas_call(functools.partial(kernel, (ns, nt, nx, nz)), out_shape=(ja...]
where the time goes in v4:
time: 79.5 us; the launch traced here: 79.3 us
  Pallas kernels  77.1 us (97%)
  other arithmetic  1.55 us (2%)
    pallas_call x1, Pallas kernels, on_device(): pl.pallas_call(functools.partial(kernel, (ns, nt, nx, nz)), out_shape=(ja...  77.1 us

profile of v4, /device:TPU:25, one launch (start us, length us, event | category | flops | bytes accessed | tf_op | source)
XLA Modules:
  0.0 79.3 jit_solution(16261542996808455548)
XLA Ops:
  0.7 77.1 %shard_map.64 = (f32[2,16,768]{2,1,0:T(8,128)}, f32[16,768]{1,0:T(8,128)}) custom-call(f32[2,2,768,768]{3,2,1,0:T(8,128)} %bitcast.9, s32[1,1]{1,0:T(1,128)S(6)} %copy.8.side_ref, s32[1,64]{1,0:T(1,128)} %bitcast.13, f32[2,64,2048]{2,1,0:T(8,128)} %bitcast.10, f32[2,64,768]{2,1,0:T(8,128)} %bitcast.11, f32[2,16,768]{2,1,0:T(8,128)} %bitcast.12), custom_call_target="tpu_custom_call" | custom-call | tf_op jit(solution)/shard_map/pallas_call | solution.py:470
  77.8 1.5 %multiply_bitcast_fusion = f32[1,2,1,16,768]{4,3,2,1,0:T(8,128)} fusion(f32[2,16,768]{2,1,0:T(8,128)} %get-tuple-element.7, f32[16,768]{1,0:T(8,128)} %get-tuple-element.8), kind=kLoop, calls=%fused_computation | loop fusion | flops 24576 | bytes 245760 | tf_op jit(solution)/shard_map/reshape | solution.py:519

commit v5 on v4

--- a/solution.py
+++ b/solution.py
@@ -110,7 +110,7 @@
         load.start()
 
     spread = [
-        (int(outward(k // nx, nz)), int(outward(k % nx, nx))) for k in range(nt)
+        (int(outward(k % nz, nz)), int(outward(k // nz, nx))) for k in range(nt)
     ]
     wrap_x = [lax.rem(my_x + dx, nx) * nz for dx in range(nx)]
     wrap_z = [lax.rem(my_z + dz, nz) for dz in range(nz)]

time: 79.5 us -> 79 us (level)
  no operation moved by 1% of the time
where the time goes in v5:
time: 79 us; the launch traced here: 78.9 us
  Pallas kernels  76.7 us (97%)
  other arithmetic  1.55 us (2%)
    pallas_call x1, Pallas kernels, on_device(): pl.pallas_call(functools.partial(kernel, (ns, nt, nx, nz)), out_shape=(ja...  76.7 us

profile of v5, /device:TPU:25, one launch (start us, length us, event | category | flops | bytes accessed | tf_op | source)
XLA Modules:
  0.0 78.9 jit_solution(2448342396011323871)
XLA Ops:
  0.7 76.7 %shard_map.64 = (f32[2,16,768]{2,1,0:T(8,128)}, f32[16,768]{1,0:T(8,128)}) custom-call(f32[2,2,768,768]{3,2,1,0:T(8,128)} %bitcast.9, s32[1,1]{1,0:T(1,128)S(6)} %copy.8.side_ref, s32[1,64]{1,0:T(1,128)} %bitcast.13, f32[2,64,2048]{2,1,0:T(8,128)} %bitcast.10, f32[2,64,768]{2,1,0:T(8,128)} %bitcast.11, f32[2,16,768]{2,1,0:T(8,128)} %bitcast.12), custom_call_target="tpu_custom_call" | custom-call | tf_op jit(solution)/shard_map/pallas_call | solution.py:470
  77.4 1.5 %multiply_bitcast_fusion = f32[1,2,1,16,768]{4,3,2,1,0:T(8,128)} fusion(f32[2,16,768]{2,1,0:T(8,128)} %get-tuple-element.7, f32[16,768]{1,0:T(8,128)} %get-tuple-element.8), kind=kLoop, calls=%fused_computation | loop fusion | flops 24576 | bytes 245760 | tf_op jit(solution)/shard_map/reshape | solution.py:519

commit v6 on v5

--- a/solution.py
+++ b/solution.py
@@ -287,36 +287,41 @@
                 nsel[slot, :, i * n : (i + 1) * n] = jnp.where(in_first, re, im).astype(BF16)
         a_v[...] = pick(src_v[...].reshape(2 * rows, tile))
 
-    def wait_u():
-        for piece in range(pieces):
-            cols = slice(piece * tile // pieces, (piece + 1) * tile // pieces)
-            for i in range(3):
-                part = u_in.at[i, :, :, cols]
-                pltpu.make_async_copy(part, part, u_recv.at[piece, i]).wait()
-
-    def incoming(slot):
-        x = u_in[2] if slot == 0 else choose(u_in[0], u_in[1])
-        return halves(x.reshape(2 * rows, tile))
-
-    def near(cols):
+    def piece_at(piece):
+        return slice(piece * tile // pieces, (piece + 1) * tile // pieces)
+
+    def wait_u(piece):
+        for i in range(3):
+            part = u_in.at[i, :, :, piece_at(piece)]
+            pltpu.make_async_copy(part, part, u_recv.at[piece, i]).wait()
+
+    def incoming(slot, span):
+        def block(i):
+            return u_in[i, :, :, span].reshape(2 * rows, span.stop - span.start)
+
+        return halves(block(2) if slot == 0 else choose(block(0), block(1)))
+
+    def near(span, cols):
         sums = [None, None]
         for slot in range(2):
-            hi, lo = incoming(slot)
+            hi, lo = incoming(slot, span)
             both = jnp.concatenate([hi, lo], axis=0)
             for part in range(2):
-                prod = mm(both, near_hi[slot, part, :, cols])
-                term = prod[: 2 * rows] + prod[2 * rows :] + mm(hi, near_lo[slot, part, :, cols])
+                prod = mm(both, near_hi[slot, part, span, cols])
+                term = prod[: 2 * rows] + prod[2 * rows :] + mm(hi, near_lo[slot, part, span, cols])
                 sums[part] = term if slot == 0 else sums[part] + term
-        n_v[0, :, cols] = sums[0][:rows] - sums[1][rows:] + src_v[0, :, cols]
-        n_v[1, :, cols] = sums[1][:rows] + sums[0][rows:] + src_v[1, :, cols]
+        return sums[0][:rows] - sums[1][rows:], sums[1][:rows] + sums[0][rows:]
 
     @pl.when(jnp.logical_not(from_far))
     def _():
         @pl.when(has_prev)
         def _():
-            wait_u()
-
-        near(slice(0, tile))
+            for piece in range(pieces):
+                wait_u(piece)
+
+        n_re, n_im = near(slice(0, tile), slice(0, tile))
+        n_v[0] = n_re + src_v[0]
+        n_v[1] = n_im + src_v[1]
         a_v[...] = pick(n_v[...].reshape(2 * rows, tile))
 
     order = [int(outward(k, nz)) for k in range(nz)][::-1]
@@ -374,19 +379,23 @@
 
     @pl.when(from_far)
     def _():
-        wait_u()
-
-        @pl.when(has_next)
-        def _():
-            total = None
-            for slot in range(2):
-                term = mm(jnp.concatenate(incoming(slot), axis=0), nsel[slot])
-                total = term if total is None else total + term
-            total = total[: 2 * rows] + total[2 * rows :]
-            total = total[:, :n] + total[:, n:]
-            turned = pltpu.roll(total[rows:], rank, 1)
-            a_v[...] += total[:rows] + jnp.where(first[:rows], -turned, turned)
-            emit(0)
+        for piece in range(pieces):
+            span = piece_at(piece)
+            wait_u(piece)
+
+            @pl.when(has_next)
+            def _():
+                total = None
+                for slot in range(2):
+                    lhs = jnp.concatenate(incoming(slot, span), axis=0)
+                    term = mm(lhs, nsel[slot, span])
+                    total = term if total is None else total + term
+                total = total[: 2 * rows] + total[2 * rows :]
+                total = total[:, :n] + total[:, n:]
+                turned = pltpu.roll(total[rows:], rank, 1)
+                a_v[...] += total[:rows] + jnp.where(first[:rows], -turned, turned)
+                if piece == pieces - 1:
+                    emit(0)
 
     wait_p(1, late)
     far_ahead(1, late, False)
@@ -404,7 +413,9 @@
 
         @pl.when(from_far)
         def _():
-            near(cols)
+            n_re, n_im = near(slice(0, tile), cols)
+            n_v[0, :, cols] = n_re + src_v[0, :, cols]
+            n_v[1, :, cols] = n_im + src_v[1, :, cols]
 
         u_out[:, :, cols] += n_v[:, :, cols]
 

time: 79 us -> 79.2 us (level)
  no operation moved by 1% of the time
where the time goes in v6:
time: 79.2 us; the launch traced here: 79.1 us
  Pallas kernels  76.9 us (97%)
  other arithmetic  1.55 us (2%)
    pallas_call x1, Pallas kernels, on_device(): pl.pallas_call(functools.partial(kernel, (ns, nt, nx, nz)), out_shape=(ja...  76.9 us

profile of v6, /device:TPU:25, one launch (start us, length us, event | category | flops | bytes accessed | tf_op | source)
XLA Modules:
  0.0 79.1 jit_solution(2945397184654962406)
XLA Ops:
  0.7 76.9 %shard_map.64 = (f32[2,16,768]{2,1,0:T(8,128)}, f32[16,768]{1,0:T(8,128)}) custom-call(f32[2,2,768,768]{3,2,1,0:T(8,128)} %bitcast.9, s32[1,1]{1,0:T(1,128)S(6)} %copy.8.side_ref, s32[1,64]{1,0:T(1,128)} %bitcast.13, f32[2,64,2048]{2,1,0:T(8,128)} %bitcast.10, f32[2,64,768]{2,1,0:T(8,128)} %bitcast.11, f32[2,16,768]{2,1,0:T(8,128)} %bitcast.12), custom_call_target="tpu_custom_call" | custom-call | tf_op jit(solution)/shard_map/pallas_call | solution.py:481
  77.5 1.5 %multiply_bitcast_fusion = f32[1,2,1,16,768]{4,3,2,1,0:T(8,128)} fusion(f32[2,16,768]{2,1,0:T(8,128)} %get-tuple-element.7, f32[16,768]{1,0:T(8,128)} %get-tuple-element.8), kind=kLoop, calls=%fused_computation | loop fusion | flops 24576 | bytes 245760 | tf_op jit(solution)/shard_map/reshape | solution.py:530
